TPU v7x, 32 devices: a whole 2x2x4 slice. The times are simulated.
32 devices in a mesh: dp: 4 (over z), fsdp: 8 (over y, x, core).
Axes of the slice: x: 2, y: 2, z: 4, core: 2. Of those that a mesh axis runs over, the one named last changes fastest.
Arguments:
- frames: bfloat16 [64, 256, 1536], P(('dp', 'fsdp')), may hold values from -6 to 6
- lengths: int32 [64], P(('dp', 'fsdp')), may hold values from 1 to 256, as said below
- norm_in_gain: float32 [1536], replicated, may hold values from 0.1 to 1.9
- w_in: bfloat16 [1536, 3072], P('fsdp'), may hold values from -0.15625 to 0.15625
- dw_kernel: float32 [31, 1536], replicated, may hold values from -1 to 1
- norm_mid_gain: float32 [1536], replicated, may hold values from 0.1 to 1.9
- w_out: bfloat16 [1536, 1536], P('fsdp'), may hold values from -0.15625 to 0.15625
Outputs:
- module_out: bfloat16 [64, 256, 1536], P(('dp', 'fsdp'))
Inputs may be any that keep to these rules, and one draw needn't show every extreme that they name: Utterance u has ceil(lengths[u] / 64) live blocks. Two devices of the same dp index whose fsdp indices differ by half of 8 hold at most 10 live blocks together; in every dp group some such pair holds exactly 10, one device of it having all 8 blocks live with every utterance of length 256.
All inputs are finite; a program needn't handle non-finite values.
Results may differ from a plain program's by a relative error of at most 0.0066.
Values may be sent and summed in bfloat16 or wider, within the bound.
A program may use at most 128 MiB of HBM per device.

v0:
```python
import jax
import jax.numpy as jnp
from jax import lax
from jax.sharding import PartitionSpec as P


def layer_norm(values, gain_vec):
    center = values - jnp.mean(values, axis=-1, keepdims=True)
    spread = jnp.mean(center * center, axis=-1, keepdims=True)
    return center * lax.rsqrt(spread + 1e-05) * gain_vec


def expand_in(flat_rows, w_in):
    model_width = flat_rows.shape[1]
    projected = jnp.dot(
        flat_rows,
        lax.all_gather(w_in, "fsdp", axis=0, tiled=True),
        preferred_element_type=jnp.float32,
    )
    return (projected[:, :model_width] * jax.nn.sigmoid(projected[:, model_width:])).astype(
        jnp.bfloat16
    )


def contract_out(flat_rows, w_out):
    projected = jnp.dot(
        flat_rows,
        lax.all_gather(w_out, "fsdp", axis=0, tiled=True),
        preferred_element_type=jnp.float32,
    )
    return projected.astype(jnp.bfloat16)


def on_device(frames, lengths, norm_in_gain, w_in, dw_kernel, norm_mid_gain, w_out):
    utt_count, frame_span, model_width = frames.shape
    positions = jnp.arange(frame_span, dtype=jnp.int32)
    valid = (positions[None, :] < lengths[:, None])[:, :, None]
    normed = layer_norm(frames.astype(jnp.float32), norm_in_gain).astype(jnp.bfloat16)

    def apply_rows(values, compute):
        return compute(values.reshape(utt_count * frame_span, model_width)).reshape(
            utt_count, frame_span, -1
        )

    def first_section(flat_rows):
        return expand_in(flat_rows, w_in)

    def last_section(flat_rows):
        return contract_out(flat_rows, w_out)

    gated = apply_rows(normed, first_section)
    gated = jnp.where(valid, gated, jnp.zeros((), jnp.bfloat16))
    taps = dw_kernel.shape[0]
    half_k = (taps - 1) // 2
    padded = jnp.pad(gated, ((0, 0), (half_k, half_k), (0, 0)))
    convolved = jnp.zeros((utt_count, frame_span, model_width), jnp.float32)
    for offset in range(taps):
        convolved = convolved + padded[:, offset : offset + frame_span, :] * dw_kernel[offset]
    middle = layer_norm(convolved, norm_mid_gain)
    middle = (middle * jax.nn.sigmoid(middle)).astype(jnp.bfloat16)
    result = apply_rows(middle, last_section)
    return jnp.where(valid, result, jnp.zeros((), jnp.bfloat16))


def solution(mesh):
    return jax.shard_map(
        on_device,
        mesh=mesh,
        in_specs=(
            P(("dp", "fsdp"), None, None),
            P(("dp", "fsdp")),
            P(),
            P("fsdp", None),
            P(),
            P(),
            P("fsdp", None),
        ),
        out_specs=P(("dp", "fsdp"), None, None),
        check_vma=False,
    )
```

profile of v0, /device:TPU:0, one launch (start us, length us, event | category | flops | bytes accessed | tf_op | source)
XLA Modules:
  0.0 124.5 jit_solution(6595838935682310830)
XLA Ops:
  6.5 0.0 all-gather.3.cloned.1.call-start
  6.5 0.7 all-gather.3.cloned.1.call-update
  7.3 0.0 all-gather.5.cloned.1.call-start
  7.3 0.7 all-gather.5.cloned.1.call-update
  8.0 1.5 %slice_reduce_fusion.29 = (f32[1536]{0:T(1024)S(1)}, f32[1536]{0:T(1024)S(1)}, f32[1536]{0:T(1024)S(1)}, f32[1536]{0:T(1024)S(1)}, f32[1536]{0:T(1024)S(1)}, /*i...) fusion(f32[31,1536]{1,0:T(8,128)} %param.11), kind=kLoop, calls=%fused_computation.56 | loop fusion | bytes 147456 | tf_op jit(solution)/shard_map/slice | solution.py:58
  9.5 2.1 %slice_reduce_fusion.30 = (f32[1536]{0:T(1024)S(1)}, f32[1536]{0:T(1024)S(1)}, f32[1536]{0:T(1024)S(1)}, f32[1536]{0:T(1024)S(1)}, f32[1536]{0:T(1024)S(1)}, /*i...) fusion(f32[31,1536]{1,0:T(8,128)} %param.11), kind=kLoop, calls=%fused_computation.57 | loop fusion | bytes 233472 | tf_op jit(solution)/shard_map/slice | solution.py:58
  11.6 0.0 copy-done
  11.6 0.3 convert_reduce_fusion
  11.9 0.0 copy-done.3
  11.9 0.1 iota_compare_fusion
  12.0 0.6 fusion.2
  12.5 0.0 copy-done.1
  12.5 0.5 fusion.4
  13.1 57.6 %all-gather.3.cloned.1.call-done = bf16[1536,3072]{1,0:T(8,128)(2,1)} async-done(((bf16[192,3072]{1,0:T(8,128)(2,1)}), bf16[1536,3072]{1,0:T(8,128)(2,1)}) %all-gather.3.cloned.1.call-update) | async-done | bytes 9437200 | tf_op jit(solution)/shard_map/all_gather | solution.py:17
  70.7 7.6 %fusion.11 = f32[512,3072]{1,0:T(8,128)S(1)} fusion(bf16[512,1536]{1,0:T(8,128)(2,1)S(1)} %bitcast.9, bf16[1536,3072]{1,0:T(8,128)(2,1)} %all-gather.3.cloned.1.call-done), kind=kOutput, calls=%fused_computation.64 | convolution fusion | flops 4831838208 | bytes 17301504 | tf_op jit(solution)/shard_map/dot_general | solution.py:15
  78.3 0.8 fusion.9
  79.1 0.2 broadcast_select_fusion.1
  79.3 0.0 copy-start.2
  79.3 13.8 %fusion.10 = (f32[2,256]{1,0:T(2,128)S(1)}, f32[2,256,1536]{2,1,0:T(8,128)S(1)}) fusion(f32[1536]{0:T(1024)S(1)} %get-tuple-element.34, f32[1536]{0:T(1024)S(1)} %get-tuple-element.35, f32[1536]{0:T(1024)S(1)} %get-tuple-element.6, f32[1536]{0:T(1024)S(1)} %get-tuple-element.7, f32[1536]{0:T(1024)S(1)} %get-tuple-element.8, f32[1536]{0:T(1024)S(1)} %get-tuple-element.9, ...), kind=kLoop, calls=%fused_computation.63 | loop fusion | flops 73137664 | bytes 4911104 | tf_op jit(solution)/shard_map/reduce_sum | solution.py:8
  93.1 0.5 multiply_reduce_fusion
  93.6 1.1 multiply_convert_fusion
  94.6 16.7 %all-gather.5.cloned.1.call-done = bf16[1536,1536]{1,0:T(8,128)(2,1)} async-done(((bf16[192,1536]{1,0:T(8,128)(2,1)}), bf16[1536,1536]{1,0:T(8,128)(2,1)}) %all-gather.5.cloned.1.call-update) | async-done | bytes 4718608 | tf_op jit(solution)/shard_map/all_gather | solution.py:28
  111.4 5.0 %convolution_convert_fusion = bf16[512,1536]{1,0:T(8,128)(2,1)S(1)} fusion(bf16[512,1536]{1,0:T(8,128)(2,1)S(1)} %bitcast.11, bf16[1536,1536]{1,0:T(8,128)(2,1)} %all-gather.5.cloned.1.call-done), kind=kOutput, calls=%fused_computation.16 | convolution fusion | flops 2416705536 | bytes 7864320 | tf_op jit(solution)/shard_map/dot_general | solution.py:26
  116.3 1.3 %broadcast_select_fusion = bf16[2,256,1536]{2,1,0:T(8,128)(2,1)} fusion(bf16[2,256,1536]{2,1,0:T(8,128)(2,1)S(1)} %bitcast.10, pred[2,256]{1,0:T(4,128)(4,1)S(1)} %iota_compare_fusion), kind=kLoop, calls=%fused_computation.25 | loop fusion | flops 786432 | bytes 3146240 | tf_op jit(solution)/shard_map/jit(_where)/select_n | solution.py:62
  (8 shorter events, 0.0 us)
Async XLA Ops:
  6.5 5.1 %copy-start = (bf16[2,256,1536]{2,1,0:T(8,128)(2,1)S(1)}, bf16[2,256,1536]{2,1,0:T(8,128)(2,1)}, u32[]{:S(2)}) copy-start(bf16[2,256,1536]{2,1,0:T(8,128)(2,1)} %param.7) | copy-start | bytes 4718596
  6.5 5.3 %copy-start.3 = (s32[2]{0:T(128)S(1)}, s32[2]{0:T(128)}, u32[]{:S(2)}) copy-start(s32[2]{0:T(128)} %param.8) | copy-start | bytes 28
  6.5 6.0 %copy-start.1 = (f32[1536]{0:T(1024)S(1)}, f32[1536]{0:T(1024)}, u32[]{:S(2)}) copy-start(f32[1536]{0:T(1024)} %param.9) | copy-start | bytes 18436
  6.5 64.1 %all-gather.3.cloned.1.call-start = ((), (), s32[]{:S(2)}) async-start(), calls=%async_computation | async-start | bytes 10616832 | tf_op jit(solution)/shard_map/all_gather | solution.py:17
  7.3 104.1 %all-gather.5.cloned.1.call-start = ((), (), s32[]{:S(2)}) async-start(), calls=%async_computation.1 | async-start | bytes 5308416 | tf_op jit(solution)/shard_map/all_gather | solution.py:28
  79.3 14.3 %copy-start.2 = (f32[1536]{0:T(1024)S(1)}, f32[1536]{0:T(1024)}, u32[]{:S(2)}) copy-start(f32[1536]{0:T(1024)} %param.12) | copy-start | bytes 18436
Sparse Core Ops, SparseCore 0:
  9.2 61.4 all-gather.2
  72.6 38.7 all-gather.4
where the time goes:
time: 125 us; the launch traced here: 124 us
  waiting for transfers between devices  75.7 us (61%)
  other arithmetic  19.1 us (15%)
  between operations  13.5 us (11%)
  matrix products  12.5 us (10%)
  local copies, waits for them, and re-layouts  3.59 us (3%)
    all_gather x1, waiting for transfers between devices, expand_in(): lax.all_gather(w_in, 'fsdp', axis=0, tiled=True)  57.6 us
    all_gather x1, waiting for transfers between devices, contract_out(): lax.all_gather(w_out, 'fsdp', axis=0, tiled=True)  16.7 us
    reduce_sum x2, other arithmetic, layer_norm(): center = values - jnp.mean(values, axis=-1, keepdims=True)  14.1 us
    dot_general x1, matrix products, expand_in(): jnp.dot(flat_rows, lax.all_gather(w_in, 'fsdp', axis=0, tiled=True), pref...  7.59 us
    dot_general x1, matrix products, contract_out(): jnp.dot(flat_rows, lax.all_gather(w_out, 'fsdp', axis=0, tiled=True), pre...  4.95 us
    slice x2, local copies, waits for them, and re-layouts, on_device(): dw_kernel[offset]  3.57 us
  transfers between devices with their start and end apart: 2, of which 2 were waited for; matrix products, arithmetic and copies ran while one was open for 23% of the time, Pallas kernels for 0%

commit v1 on v0

--- a/solution.py
+++ b/solution.py
@@ -12,11 +12,29 @@
 
 def expand_in(flat_rows, w_in):
     model_width = flat_rows.shape[1]
-    projected = jnp.dot(
-        flat_rows,
-        lax.all_gather(w_in, "fsdp", axis=0, tiled=True),
-        preferred_element_type=jnp.float32,
-    )
+
+    def extend_target(chunk):
+        axis_id = "fsdp"
+        even = lax.axis_size(axis_id)
+        piece_now = lax.axis_index(axis_id)
+        g_now, e_next, tmp = (even, piece_now, chunk.shape[0])
+        views = tuple(((tick, (tick + 1) % g_now) for tick in range(g_now)))
+        nodes = tuple(((tick, (tick - 1) % g_now) for tick in range(g_now)))
+        odd = jnp.zeros((*chunk.shape[:0], g_now * tmp, *chunk.shape[1:]), chunk.dtype)
+        odd = lax.dynamic_update_slice_in_dim(odd, chunk, e_next * tmp, axis=0)
+        placed = inter = chunk
+        z = g_now // 2
+        for kk in tuple(range(1, z + 1)):
+            placed = lax.ppermute(placed, axis_id, views)
+            odd = lax.dynamic_update_slice_in_dim(odd, placed, (e_next - kk) % g_now * tmp, axis=0)
+            if kk < g_now - z:
+                inter = lax.ppermute(inter, axis_id, nodes)
+                odd = lax.dynamic_update_slice_in_dim(
+                    odd, inter, (e_next + kk) % g_now * tmp, axis=0
+                )
+        return odd
+
+    projected = jnp.dot(flat_rows, extend_target(w_in), preferred_element_type=jnp.float32)
     return (projected[:, :model_width] * jax.nn.sigmoid(projected[:, model_width:])).astype(
         jnp.bfloat16
     )

time: 125 us -> 159 us (1.27)
  waiting for transfers between devices: 75.7 us -> 97.7 us
  starting transfers between devices: 0.04 us -> 9.81 us
  matrix products: 12.5 us -> 9.97 us
  local copies, waits for them, and re-layouts: 3.59 us -> 5.35 us
    ppermute x0 -> x7, waiting for transfers between devices: none -> 97.6 us  [the longest x4 94.1 us: extend_target(): placed = lax.ppermute(placed, axis_id, views)]
    all_gather x1 -> x0, waiting for transfers between devices: 57.6 us -> none  [expand_in(): lax.all_gather(w_in, 'fsdp', axis=0, tiled=True)]
    all_gather x1, waiting for transfers between devices: 16.7 us -> 0.02 us  [contract_out(): lax.all_gather(w_out, 'fsdp', axis=0, tiled=True)]
    ppermute x0 -> x7, starting transfers between devices: none -> 9.81 us  [the longest x3 8.38 us: extend_target(): inter = lax.ppermute(inter, axis_id, nodes)]
    dynamic_update_slice x0 -> x8, local copies, waits for them, and re-layouts: none -> 3.57 us  [the longest x4 3.06 us: extend_target(): lax.dynamic_update_slice_in_dim(odd, placed, (e_next - kk) % g_now * tmp,...]
    slice x2, local copies, waits for them, and re-layouts: 3.57 us -> 0.5 us  [on_device(): dw_kernel[offset]]
    dot_general x1, matrix products: 7.59 us -> 5.04 us  [expand_in(): jnp.dot(flat_rows, extend_target(w_in), preferred_element_type=jnp.float32)]
  transfers between devices with their start and end apart: 2 -> 8, of which waited for: 2 -> 6; matrix products, arithmetic and copies ran while one was open for 23% -> 19% of each run, Pallas kernels for 0% -> 0%
where the time goes in v1:
time: 159 us; the launch traced here: 157 us
  waiting for transfers between devices  97.7 us (61%)
  other arithmetic  20.5 us (13%)
  between operations  13.7 us (9%)
  matrix products  9.97 us (6%)
  starting transfers between devices  9.81 us (6%)
  local copies, waits for them, and re-layouts  5.35 us (3%)
    ppermute x4, waiting for transfers between devices, extend_target(): placed = lax.ppermute(placed, axis_id, views)  94.1 us
    reduce_sum x2, other arithmetic, layer_norm(): center = values - jnp.mean(values, axis=-1, keepdims=True)  15.5 us
    ppermute x3, starting transfers between devices, extend_target(): inter = lax.ppermute(inter, axis_id, nodes)  8.38 us
    dot_general x1, matrix products, expand_in(): jnp.dot(flat_rows, extend_target(w_in), preferred_element_type=jnp.float32)  5.04 us
    dot_general x1, matrix products, contract_out(): jnp.dot(flat_rows, lax.all_gather(w_out, 'fsdp', axis=0, tiled=True), pre...  4.93 us
    ppermute x3, waiting for transfers between devices, extend_target(): inter = lax.ppermute(inter, axis_id, nodes)  3.52 us
  transfers between devices with their start and end apart: 8, of which 6 were waited for; matrix products, arithmetic and copies ran while one was open for 19% of the time, Pallas kernels for 0%

profile of v1, /device:TPU:0, one launch (start us, length us, event | category | flops | bytes accessed | tf_op | source)
XLA Modules:
  0.0 157.1 jit_solution(100113233877723067)
XLA Ops:
  6.5 0.5 collective-permute-start
  7.0 2.9 %collective-permute-start.1 = (bf16[192,3072]{1,0:T(8,128)(2,1)}, bf16[192,3072]{1,0:T(8,128)(2,1)S(1)}, u32[]{:S(2)}, u32[]{:S(2)}) collective-permute-start(bf16[192,3072]{1,0:T(8,128)(2,1)} %param.10), channel_id=1, source_target_pairs={{0,7},{1,0},{2,1},{3,2},{4,3},{5,4},{6,5},{7,6},{8,15},{9,8},{10,9... | collective-permute-start | bytes 3538952 | tf_op jit(solution)/shard_map/ppermute | solution.py:31
  10.0 1.7 %convert_reduce_fusion = f32[2,256]{1,0:T(2,128)S(1)} fusion(bf16[2,256,1536]{2,1,0:T(8,128)(2,1)} %param.7), kind=kLoop, calls=%fused_computation.1 | loop fusion | flops 1572352 | bytes 1574912 | tf_op jit(solution)/shard_map/reduce_sum | solution.py:8
  11.7 28.7 %collective-permute-done = bf16[192,3072]{1,0:T(8,128)(2,1)} collective-permute-done((bf16[192,3072]{1,0:T(8,128)(2,1)}, bf16[192,3072]{1,0:T(8,128)(2,1)}, u32[]{:S(2)}, u32[]{:S(2)}) %collective-permute-start) | collective-permute-done | bytes 1179680 | tf_op jit(solution)/shard_map/ppermute | solution.py:28
  40.5 0.9 collective-permute-start.2
  41.4 0.5 fusion.2
  42.1 0.5 fusion.4
  42.6 1.7 %collective-permute-done.1 = bf16[192,3072]{1,0:T(8,128)(2,1)S(1)} collective-permute-done((bf16[192,3072]{1,0:T(8,128)(2,1)}, bf16[192,3072]{1,0:T(8,128)(2,1)S(1)}, u32[]{:S(2)}, u32[]{:S(2)}) %collective-permute-start.1) | collective-permute-done | bytes 1179680 | tf_op jit(solution)/shard_map/ppermute | solution.py:31
  44.4 2.8 %collective-permute-start.3 = (bf16[192,3072]{1,0:T(8,128)(2,1)S(1)}, bf16[192,3072]{1,0:T(8,128)(2,1)S(1)}, u32[]{:S(2)}, u32[]{:S(2)}) collective-permute-start(bf16[192,3072]{1,0:T(8,128)(2,1)S(1)} %collective-permute-done.1), channel_id=1, source_target_pairs={{0,7},{1,0},{2,1},{3,2},{4,3},{5,4},{6,5},{7,6},{8,15},{9,8},{10,9... | collective-permute-start | bytes 3538952 | tf_op jit(solution)/shard_map/ppermute | solution.py:31
  47.5 32.7 %collective-permute-done.2 = bf16[192,3072]{1,0:T(8,128)(2,1)} collective-permute-done((bf16[192,3072]{1,0:T(8,128)(2,1)}, bf16[192,3072]{1,0:T(8,128)(2,1)}, u32[]{:S(2)}, u32[]{:S(2)}) %collective-permute-start.2) | collective-permute-done | bytes 1179680 | tf_op jit(solution)/shard_map/ppermute | solution.py:28
  80.4 1.2 broadcast_in_dim.29
  81.8 1.4 constant_dynamic-update-slice_fusion.6
  83.2 2.7 %collective-permute-start.5 = (bf16[192,3072]{1,0:T(8,128)(2,1)S(1)}, bf16[192,3072]{1,0:T(8,128)(2,1)S(1)}, u32[]{:S(2)}, u32[]{:S(2)}) collective-permute-start(bf16[192,3072]{1,0:T(8,128)(2,1)S(1)} %collective-permute-done.3), channel_id=1, source_target_pairs={{0,7},{1,0},{2,1},{3,2},{4,3},{5,4},{6,5},{7,6},{8,15},{9,8},{10,9... | collective-permute-start | bytes 3538952 | tf_op jit(solution)/shard_map/ppermute | solution.py:31
  86.1 19.8 %collective-permute-done.4 = bf16[192,3072]{1,0:T(8,128)(2,1)S(1)} collective-permute-done((bf16[192,3072]{1,0:T(8,128)(2,1)}, bf16[192,3072]{1,0:T(8,128)(2,1)S(1)}, u32[]{:S(2)}, u32[]{:S(2)}) %collective-permute-start.4) | collective-permute-done | bytes 1179680 | tf_op jit(solution)/shard_map/ppermute | solution.py:28
  105.9 1.4 constant_dynamic-update-slice_fusion.4
  107.5 1.8 %collective-permute-done.5 = bf16[192,3072]{1,0:T(8,128)(2,1)S(1)} collective-permute-done((bf16[192,3072]{1,0:T(8,128)(2,1)S(1)}, bf16[192,3072]{1,0:T(8,128)(2,1)S(1)}, u32[]{:S(2)}, u32[]{:S(2)}) %collective-permute-start.5) | collective-permute-done | bytes 1179680 | tf_op jit(solution)/shard_map/ppermute | solution.py:31
  109.5 12.9 %collective-permute-done.6 = bf16[192,3072]{1,0:T(8,128)(2,1)S(1)} collective-permute-done((bf16[192,3072]{1,0:T(8,128)(2,1)S(1)}, bf16[192,3072]{1,0:T(8,128)(2,1)S(1)}, u32[]{:S(2)}, u32[]{:S(2)}) %collective-permute-start.6) | collective-permute-done | bytes 1179680 | tf_op jit(solution)/shard_map/ppermute | solution.py:28
  122.5 5.0 %fusion.11 = f32[512,3072]{1,0:T(8,128)S(1)} fusion(bf16[512,1536]{1,0:T(8,128)(2,1)S(1)} %bitcast.9, bf16[1536,3072]{1,0:T(8,128)(2,1)S(1)} %constant_dynamic-update-slice_fusion), kind=kOutput, calls=%fused_computation.72 | convolution fusion | flops 4831838208 | bytes 17301504 | tf_op jit(solution)/shard_map/dot_general | solution.py:37
  127.6 0.8 fusion.9
  128.6 13.8 %fusion.10 = (f32[2,256]{1,0:T(2,128)S(1)}, f32[2,256,1536]{2,1,0:T(8,128)S(1)}) fusion(f32[1536]{0:T(1024)S(1)} %get-tuple-element.34, f32[1536]{0:T(1024)S(1)} %get-tuple-element.35, f32[1536]{0:T(1024)S(1)} %get-tuple-element.6, f32[1536]{0:T(1024)S(1)} %get-tuple-element.7, f32[1536]{0:T(1024)S(1)} %get-tuple-element.8, f32[1536]{0:T(1024)S(1)} %get-tuple-element.9, ...), kind=kLoop, calls=%fused_computation.71 | loop fusion | flops 73137664 | bytes 4911104 | tf_op jit(solution)/shard_map/reduce_sum | solution.py:8
  142.4 0.4 multiply_reduce_fusion
  142.8 1.1 multiply_convert_fusion
  144.0 4.9 %convolution_convert_fusion = bf16[512,1536]{1,0:T(8,128)(2,1)S(1)} fusion(bf16[512,1536]{1,0:T(8,128)(2,1)S(1)} %bitcast.11, bf16[1536,1536]{1,0:T(8,128)(2,1)} %all-gather.2.cloned.1.call-done), kind=kOutput, calls=%fused_computation.16 | convolution fusion | flops 2416705536 | bytes 7864320 | tf_op jit(solution)/shard_map/dot_general | solution.py:44
  148.9 1.3 broadcast_select_fusion
  (32 shorter events, 1.7 us)
Async XLA Ops:
  6.5 34.9 %copy-start = (bf16[2,256,1536]{2,1,0:T(8,128)(2,1)S(1)}, bf16[2,256,1536]{2,1,0:T(8,128)(2,1)}, u32[]{:S(2)}) copy-start(bf16[2,256,1536]{2,1,0:T(8,128)(2,1)} %param.7) | copy-start | bytes 4718596
  6.5 35.6 %copy-start.3 = (f32[1536]{0:T(1024)S(1)}, f32[1536]{0:T(1024)}, u32[]{:S(2)}) copy-start(f32[1536]{0:T(1024)} %param.9) | copy-start | bytes 18436
  6.5 137.4 %all-gather.2.cloned.1.call-start = ((), (), s32[]{:S(2)}) async-start(), calls=%async_computation | async-start | bytes 5308416 | tf_op jit(solution)/shard_map/all_gather | solution.py:46
  6.5 33.9 %collective-permute-start = (bf16[192,3072]{1,0:T(8,128)(2,1)}, bf16[192,3072]{1,0:T(8,128)(2,1)}, u32[]{:S(2)}, u32[]{:S(2)}) collective-permute-start(bf16[192,3072]{1,0:T(8,128)(2,1)} %param.10), channel_id=1, source_target_pairs={{0,1},{1,2},{2,3},{3,4},{4,5},{5,6},{6,7},{7,0},{8,9},{9,10},{10,1... | collective-permute-start | bytes 3538952 | tf_op jit(solution)/shard_map/ppermute | solution.py:28
  7.0 37.3 %collective-permute-start.1 = (bf16[192,3072]{1,0:T(8,128)(2,1)}, bf16[192,3072]{1,0:T(8,128)(2,1)S(1)}, u32[]{:S(2)}, u32[]{:S(2)}) collective-permute-start(bf16[192,3072]{1,0:T(8,128)(2,1)} %param.10), channel_id=1, source_target_pairs={{0,7},{1,0},{2,1},{3,2},{4,3},{5,4},{6,5},{7,6},{8,15},{9,8},{10,9... | collective-permute-start | bytes 3538952 | tf_op jit(solution)/shard_map/ppermute | solution.py:31
  10.0 37.1 %copy-start.2 = (f32[31,1536]{1,0:T(8,128)S(1)}, f32[31,1536]{1,0:T(8,128)}, u32[]{:S(2)}) copy-start(f32[31,1536]{1,0:T(8,128)} %param.11) | copy-start | bytes 571396
  10.0 37.4 %copy-start.5 = (s32[2]{0:T(128)S(1)}, s32[2]{0:T(128)}, u32[]{:S(2)}) copy-start(s32[2]{0:T(128)} %param.8) | copy-start | bytes 28
  40.5 39.8 %collective-permute-start.2 = (bf16[192,3072]{1,0:T(8,128)(2,1)}, bf16[192,3072]{1,0:T(8,128)(2,1)}, u32[]{:S(2)}, u32[]{:S(2)}) collective-permute-start(bf16[192,3072]{1,0:T(8,128)(2,1)} %collective-permute-done), channel_id=1, source_target_pairs={{0,1},{1,2},{2,3},{3,4},{4,5},{5,6},{6,7},{7,0},{8,9},{9,10},{10,1... | collective-permute-start | bytes 3538952 | tf_op jit(solution)/shard_map/ppermute | solution.py:28
  44.4 38.9 %collective-permute-start.3 = (bf16[192,3072]{1,0:T(8,128)(2,1)S(1)}, bf16[192,3072]{1,0:T(8,128)(2,1)S(1)}, u32[]{:S(2)}, u32[]{:S(2)}) collective-permute-start(bf16[192,3072]{1,0:T(8,128)(2,1)S(1)} %collective-permute-done.1), channel_id=1, source_target_pairs={{0,7},{1,0},{2,1},{3,2},{4,3},{5,4},{6,5},{7,6},{8,15},{9,8},{10,9... | collective-permute-start | bytes 3538952 | tf_op jit(solution)/shard_map/ppermute | solution.py:31
  80.2 25.6 %collective-permute-start.4 = (bf16[192,3072]{1,0:T(8,128)(2,1)}, bf16[192,3072]{1,0:T(8,128)(2,1)S(1)}, u32[]{:S(2)}, u32[]{:S(2)}) collective-permute-start(bf16[192,3072]{1,0:T(8,128)(2,1)} %collective-permute-done.2), channel_id=1, source_target_pairs={{0,1},{1,2},{2,3},{3,4},{4,5},{5,6},{6,7},{7,0},{8,9},{9,10},{10,1... | collective-permute-start | bytes 3538952 | tf_op jit(solution)/shard_map/ppermute | solution.py:28
  80.4 1.3 copy-start.1
  83.2 26.1 %collective-permute-start.5 = (bf16[192,3072]{1,0:T(8,128)(2,1)S(1)}, bf16[192,3072]{1,0:T(8,128)(2,1)S(1)}, u32[]{:S(2)}, u32[]{:S(2)}) collective-permute-start(bf16[192,3072]{1,0:T(8,128)(2,1)S(1)} %collective-permute-done.3), channel_id=1, source_target_pairs={{0,7},{1,0},{2,1},{3,2},{4,3},{5,4},{6,5},{7,6},{8,15},{9,8},{10,9... | collective-permute-start | bytes 3538952 | tf_op jit(solution)/shard_map/ppermute | solution.py:31
  105.9 16.5 %collective-permute-start.6 = (bf16[192,3072]{1,0:T(8,128)(2,1)S(1)}, bf16[192,3072]{1,0:T(8,128)(2,1)S(1)}, u32[]{:S(2)}, u32[]{:S(2)}) collective-permute-start(bf16[192,3072]{1,0:T(8,128)(2,1)S(1)} %collective-permute-done.4), channel_id=1, source_target_pairs={{0,1},{1,2},{2,3},{3,4},{4,5},{5,6},{6,7},{7,0},{8,9},{9,10},{10,1... | collective-permute-start | bytes 3538952 | tf_op jit(solution)/shard_map/ppermute | solution.py:28
  128.6 14.3 %copy-start.4 = (f32[1536]{0:T(1024)S(1)}, f32[1536]{0:T(1024)}, u32[]{:S(2)}) copy-start(f32[1536]{0:T(1024)} %param.12) | copy-start | bytes 18436
Sparse Core Ops, SparseCore 0:
  10.1 56.1 all-gather.1
